TPU v7x, 512 devices: a whole 4x8x8 slice. The times are simulated.
512 devices in a mesh: dp: 4 (over z_lo, core), ctx: 32 (over z_hi, y), tp: 4 (over x).
Axes of the slice: x: 4, y: 8, z: 8 (z_hi: 4, z_lo: 2; z = z_hi * 2 + z_lo), core: 2. Of those that a mesh axis runs over, the one named last changes fastest.
Arguments:
- queries: bfloat16 [16384, 4096], P(('dp', 'ctx'), 'tp'), parts along dimension 0, may hold values from -40 to 40
- keys: bfloat16 [16384, 4096], P(('dp', 'ctx'), 'tp'), parts along dimension 0, may hold values from -40 to 40
- values: bfloat16 [16384, 4096], P(('dp', 'ctx'), 'tp'), parts along dimension 0, may hold values from -6 to 6
- query_gain: float32 [4096], P('tp'), may hold values from 0.1 to 1.9
- key_gain: float32 [4096], P('tp'), may hold values from 0.1 to 1.9
- block_mask: int32 [32, 32], P('ctx'), may hold values from 0 to 1, as said below
Outputs:
- attended: bfloat16 [16384, 4096], P(('dp', 'ctx'), 'tp'), parts along dimension 0
There are 4 independent parts, one for each index of `dp`. A program takes and returns all parts, laid end to end along the dimension named above; an argument that names none is the same for every part. Nothing has to cross between parts.
Inputs may be any that keep to these rules, and one draw needn't show every extreme that they name: block_mask[i, i] is 1 for every i, and block_mask[i, j] is 0 unless |i - j| is a power of two.
All inputs are finite; a program needn't handle non-finite values.
Results may differ from a plain program's by a relative error of at most 0.011.
Values may be sent and summed in bfloat16 or wider, within the bound.
No kernel may reach another device: no remote copies, remote signals or barrier semaphores. Data moves between devices by JAX's collectives and lax.ppermute only.
A program may use at most 128 MiB of HBM per device.

v0:
```python
import jax
import jax.numpy as jnp
from jax import lax
from jax.sharding import PartitionSpec as P

HEADS = 32
HD = 128
BLOCK = 128
epsilon = 1e-06
floor_score = -1e30


def normalize(raw_rows, total_sq, gain_vec, full_width):
    as_float = raw_rows.astype(jnp.float32)
    factor = lax.rsqrt(total_sq / full_width + epsilon)
    return (as_float * factor[:, None] * gain_vec[None, :]).astype(jnp.bfloat16)


def expand_mask(mask_part, block_len):
    q_blocks, k_blocks = mask_part.shape
    spread_out = jnp.broadcast_to(
        mask_part[:, None, :, None], (q_blocks, block_len, k_blocks, block_len)
    )
    return spread_out.reshape(q_blocks * block_len, k_blocks * block_len) > 0


def local(queries, keys, values, query_gain, key_gain, block_mask):
    tok_rows, row_width = queries.shape
    head_count = row_width // HD
    sq_queries = jnp.sum(jnp.square(queries.astype(jnp.float32)), axis=1)
    sq_keys = jnp.sum(jnp.square(keys.astype(jnp.float32)), axis=1)
    tot_queries, tot_keys = lax.psum((sq_queries, sq_keys), "tp")
    full_width = HEADS * HD
    q_normed = normalize(queries, tot_queries, query_gain, full_width).reshape(
        tok_rows, head_count, HD
    )
    k_normed = normalize(keys, tot_keys, key_gain, full_width).reshape(tok_rows, head_count, HD)
    v_heads = values.reshape(tok_rows, head_count, HD)
    score_scale = HD ** (-0.5)
    key_piece = lax.all_gather(k_normed, "ctx", axis=0, tiled=True)
    value_piece = lax.all_gather(v_heads, "ctx", axis=0, tiled=True)
    run_max = jnp.full((head_count, tok_rows), floor_score, jnp.float32)
    run_acc = jnp.zeros((tok_rows, head_count, HD), jnp.float32)
    allowed = expand_mask(block_mask, BLOCK)[None]
    scores = (
        jnp.einsum("qhd,khd->hqk", q_normed, key_piece, preferred_element_type=jnp.float32)
        * score_scale
    )
    scores = jnp.where(allowed, scores, floor_score)
    new_max = jnp.maximum(run_max, jnp.max(scores, axis=2))
    shrink = jnp.exp(run_max - new_max)
    weights = jnp.where(allowed, jnp.exp(scores - new_max[:, :, None]), 0.0)
    new_sum = jnp.sum(weights, axis=2)
    update = jnp.einsum(
        "hqk,khd->qhd",
        weights.astype(jnp.bfloat16),
        value_piece,
        preferred_element_type=jnp.float32,
    )
    new_acc = run_acc * shrink.T[:, :, None] + update
    result = new_acc / new_sum.T[:, :, None]
    return result.astype(jnp.bfloat16).reshape(tok_rows, row_width)


def solution(mesh):
    in_specs = (
        P(("dp", "ctx"), "tp"),
        P(("dp", "ctx"), "tp"),
        P(("dp", "ctx"), "tp"),
        P("tp"),
        P("tp"),
        P("ctx", None),
    )
    out_specs = P(("dp", "ctx"), "tp")
    return jax.shard_map(local, mesh=mesh, in_specs=in_specs, out_specs=out_specs, check_vma=False)
```

profile of v0, /device:TPU:2, one launch (start us, length us, event | category | flops | bytes accessed | tf_op | source)
XLA Modules:
  0.0 330.6 jit_solution(13819743713990285720)
XLA Ops:
  6.5 0.0 all-gather.3.cloned.1.call-start
  6.5 1.1 copy.10
  7.7 0.2 fusion.21
  7.8 1.1 fusion.18
  8.9 13.6 %all-reduce = (f32[128]{0:T(128)S(1)}, f32[128]{0:T(128)S(1)}) all-reduce(f32[128]{0:T(128)S(1)} %fusion.21, f32[128]{0:T(128)S(1)} %fusion.18), channel_id=1, replica_groups=mesh['dp'=4,'ctx'=32,'tp'=4] {'tp'}, use_global_device_ids=true, to_apply=%region_3.0 | all-reduce | flops 256 | bytes 2048 | tf_op jit(solution)/shard_map/psum | solution.py:32
  22.5 0.9 fusion.23
  23.4 0.8 copy.11
  24.2 0.0 all-gather.3.cloned.1.call-update
  24.3 0.0 all-gather.5.cloned.1.call-start
  24.3 1.8 copy.13
  26.1 0.0 all-gather.5.cloned.1.call-update
  26.2 0.7 compare_bitcast_fusion
  26.8 0.1 broadcast_bitcast_fusion
  26.9 137.1 %all-gather.3.cloned.1.call-done = bf16[4096,8,128]{2,0,1:T(8,128)(2,1)} async-done(((bf16[128,8,128]{2,0,1:T(8,128)(2,1)}), bf16[4096,8,128]{2,0,1:T(8,128)(2,1)}) %all-gather.3.cloned.1.call-update) | async-done | bytes 8388624 | tf_op jit(solution)/shard_map/all_gather | solution.py:40
  164.0 11.7 %fusion = (f32[8,128]{1,0:T(8,128)S(1)}, f32[8,128,4096]{2,1,0:T(8,128)}) fusion(pred[4096]{0:T(1024)(128)(4,1)S(1)} %broadcast_bitcast_fusion, bf16[4096,8,128]{2,0,1:T(8,128)(2,1)} %all-gather.3.cloned.1.call-done, bf16[128,1024]{1,0:T(8,128)(2,1)} %param.6, f32[1024]{0:T(1024)} %param.9, f32[128]{0:T(128)S(1)} %add_rsqrt_fusion.1), kind=kOutput, calls=%fused_computation.2 | convolution fusion | flops 1086848000 | bytes 25440768 | tf_op jit(solution)/shard_map/qhd,khd->hqk/dot_general | solution.py:46
  175.7 8.5 %fusion.1 = f32[8,128]{1,0:T(8,128)S(1)} fusion(f32[8,128,4096]{2,1,0:T(8,128)} %get-tuple-element.10, f32[8,128]{1,0:T(8,128)S(1)} %get-tuple-element.8, pred[4096]{0:T(1024)(128)(4,1)S(1)} %broadcast_bitcast_fusion), kind=kLoop, calls=%fused_computation.3 | loop fusion | flops 20970496 | bytes 16789504 | tf_op jit(solution)/shard_map/reduce_sum | solution.py:53
  184.2 128.0 %all-gather.5.cloned.1.call-done = bf16[4096,8,128]{0,2,1:T(8,128)(2,1)} async-done(((bf16[128,8,128]{0,2,1:T(8,128)(2,1)}), bf16[4096,8,128]{0,2,1:T(8,128)(2,1)}) %all-gather.5.cloned.1.call-update) | async-done | bytes 8388624 | tf_op jit(solution)/shard_map/all_gather | solution.py:41
  312.2 10.6 %fusion.15 = bf16[128,8,128]{0,2,1:T(8,128)(2,1)S(1)} fusion(bf16[4096,8,128]{0,2,1:T(8,128)(2,1)} %all-gather.5.cloned.1.call-done, f32[8,128,4096]{2,1,0:T(8,128)} %get-tuple-element.10, f32[8,128]{1,0:T(8,128)S(1)} %get-tuple-element.8, pred[4096]{0:T(1024)(128)(4,1)S(1)} %broadcast_bitcast_fusion, f32[128,8]{0,1:T(8,128)S(1)} %bitcast.32, ...), kind=kOutput, calls=%fused_computation.10 | convolution fusion | flops 1095106560 | bytes 25444352 | tf_op jit(solution)/shard_map/hqk,khd->qhd/dot_general | solution.py:54
  322.9 0.8 copy.14
  (3 shorter events, 0.0 us)
Async XLA Ops:
  6.5 157.4 %all-gather.3.cloned.1.call-start = ((), (), s32[]{:S(2)}) async-start(), calls=%async_computation | async-start | bytes 8650752 | tf_op jit(solution)/shard_map/all_gather | solution.py:40
  24.3 288.0 %all-gather.5.cloned.1.call-start = ((), (), s32[]{:S(2)}) async-start(), calls=%async_computation.1 | async-start | bytes 8650752 | tf_op jit(solution)/shard_map/all_gather | solution.py:41
Sparse Core Ops, SparseCore 0:
  24.4 139.5 all-gather.2
  167.0 145.1 all-gather.4
where the time goes:
time: 331 us
  waiting for transfers between devices  265 us (80%)
  matrix products  22.3 us (7%)
  blocking collectives  13.6 us (4%)
  between operations  13.4 us (4%)
  other arithmetic  11.3 us (3%)
  local copies, waits for them, and re-layouts  4.67 us (1%)
    all_gather x1, waiting for transfers between devices, local(): key_piece = lax.all_gather(k_normed, 'ctx', axis=0, tiled=True)  137 us
    all_gather x1, waiting for transfers between devices, local(): value_piece = lax.all_gather(v_heads, 'ctx', axis=0, tiled=True)  128 us
    psum x1, blocking collectives, local(): tot_queries, tot_keys = lax.psum((sq_queries, sq_keys), 'tp')  13.6 us
    dot_general x1, matrix products, local(): jnp.einsum('qhd,khd->hqk', q_normed, key_piece, preferred_element_type=jn...  11.7 us
    dot_general x1, matrix products, local(): jnp.einsum('hqk,khd->qhd', weights.astype(jnp.bfloat16), value_piece, pre...  10.6 us
    reduce_sum x1, other arithmetic, local(): new_sum = jnp.sum(weights, axis=2)  8.51 us
  transfers between devices with their start and end apart: 2, of which 2 were waited for; matrix products, arithmetic and copies ran while one was open for 7% of the time, Pallas kernels for 0%

commit v1 on v0

--- a/solution.py
+++ b/solution.py
@@ -38,7 +38,10 @@
     v_heads = values.reshape(tok_rows, head_count, HD)
     score_scale = HD ** (-0.5)
     key_piece = lax.all_gather(k_normed, "ctx", axis=0, tiled=True)
-    value_piece = lax.all_gather(v_heads, "ctx", axis=0, tiled=True)
+    devices = lax.axis_size("ctx")
+    tiles = jnp.stack([v_heads for _ in range(devices)])
+    tiles = lax.all_to_all(tiles, "ctx", split_axis=0, concat_axis=0)
+    value_piece = jnp.concatenate(tiles, axis=0)
     run_max = jnp.full((head_count, tok_rows), floor_score, jnp.float32)
     run_acc = jnp.zeros((tok_rows, head_count, HD), jnp.float32)
     allowed = expand_mask(block_mask, BLOCK)[None]

time: 331 us -> 463 us (1.40)
  the two profiles are of different devices: /device:TPU:2 before, /device:TPU:24 now
where the time goes in v1:
time: 463 us
  waiting for transfers between devices  381 us (82%)
  matrix products  22.1 us (5%)
  starting transfers between devices  16 us (3%)
  between operations  13.5 us (3%)
  other arithmetic  10.5 us (2%)
  blocking collectives  10.5 us (2%)
  local copies, waits for them, and re-layouts  9.38 us (2%)
    all_gather x1, waiting for transfers between devices, local(): key_piece = lax.all_gather(k_normed, 'ctx', axis=0, tiled=True)  381 us
    all_to_all x1, starting transfers between devices, local(): tiles = lax.all_to_all(tiles, 'ctx', split_axis=0, concat_axis=0)  16 us
    dot_general x1, matrix products, local(): jnp.einsum('qhd,khd->hqk', q_normed, key_piece, preferred_element_type=jn...  11.6 us
    psum x1, blocking collectives, local(): tot_queries, tot_keys = lax.psum((sq_queries, sq_keys), 'tp')  10.5 us
    dot_general x1, matrix products, local(): jnp.einsum('hqk,khd->qhd', weights.astype(jnp.bfloat16), value_piece, pre...  10.5 us
  transfers between devices with their start and end apart: 2, of which 1 were waited for; matrix products, arithmetic and copies ran while one was open for 6% of the time, Pallas kernels for 0%

profile of v1, /device:TPU:24, one launch (start us, length us, event | category | flops | bytes accessed | tf_op | source)
XLA Modules:
  0.0 462.7 jit_solution(4598111647328410270)
XLA Ops:
  6.5 0.0 copy-start
  6.5 0.0 copy-start.2
  6.5 0.0 copy-start.1
  6.5 0.0 all-gather.2.cloned.1.call-start
  6.5 1.1 fusion.31
  7.7 1.1 copy.15
  8.8 0.2 fusion.34
  9.0 10.5 %all-reduce = (f32[128]{0:T(128)S(1)}, f32[128]{0:T(128)S(1)}) all-reduce(f32[128]{0:T(128)S(1)} %fusion.34, f32[128]{0:T(128)S(1)} %fusion.31), channel_id=1, replica_groups=mesh['dp'=4,'ctx'=32,'tp'=4] {'tp'}, use_global_device_ids=true, to_apply=%region_3.0 | all-reduce | flops 256 | bytes 2048 | tf_op jit(solution)/shard_map/psum | solution.py:32
  19.5 0.9 fusion.36
  20.4 0.9 copy.16
  21.2 0.0 all-gather.2.cloned.1.call-update
  21.2 1.1 copy.21
  22.4 5.4 %stack.3 = bf16[32,128,8,128]{1,3,2,0:T(8,128)(2,1)} broadcast(bf16[128,8,128]{0,2,1:T(8,128)(2,1)S(1)} %bitcast.43), dimensions={1,2,3} | broadcast | bytes 8650752 | tf_op jit(solution)/shard_map/stack | solution.py:42
  27.7 16.0 %all-to-all-start = ((bf16[32,128,8,128]{1,3,2,0:T(8,128)(2,1)}), bf16[32,128,8,128]{1,3,2,0:T(8,128)(2,1)}, u32[]{:S(2)}, u32[]{:S(2)}) async-start(bf16[32,128,8,128]{1,3,2,0:T(8,128)(2,1)} %stack.3), calls=%async_computation | async-start | bytes 16777216 | tf_op jit(solution)/shard_map/all_to_all | solution.py:43
  43.7 0.0 copy-done.2
  43.8 0.1 broadcast_bitcast_fusion
  43.8 380.7 %all-gather.2.cloned.1.call-done = bf16[4096,8,128]{2,0,1:T(8,128)(2,1)} async-done(((bf16[128,8,128]{2,0,1:T(8,128)(2,1)}), bf16[4096,8,128]{2,0,1:T(8,128)(2,1)}) %all-gather.2.cloned.1.call-update) | async-done | bytes 8388624 | tf_op jit(solution)/shard_map/all_gather | solution.py:40
  424.6 0.0 copy-done
  424.6 0.0 copy-done.1
  424.6 11.6 %fusion = (f32[8,128]{1,0:T(8,128)S(1)}, f32[8,128,4096]{2,1,0:T(8,128)}) fusion(pred[4096]{0:T(1024)(128)(4,1)S(1)} %broadcast_bitcast_fusion, bf16[4096,8,128]{2,0,1:T(8,128)(2,1)} %all-gather.2.cloned.1.call-done, bf16[128,1024]{1,0:T(8,128)(2,1)S(1)} %copy-done, f32[1024]{0:T(1024)S(1)} %copy-done.1, f32[128]{0:T(128)S(1)} %add_rsqrt_fusion.1), kind=kOutput, calls=%fused_computation.2 | convolution fusion | flops 1086848000 | bytes 25440768 | tf_op jit(solution)/shard_map/qhd,khd->hqk/dot_general | solution.py:49
  436.2 8.3 %fusion.1 = f32[8,128]{1,0:T(8,128)S(1)} fusion(f32[8,128,4096]{2,1,0:T(8,128)} %get-tuple-element.10, f32[8,128]{1,0:T(8,128)S(1)} %get-tuple-element.8, pred[4096]{0:T(1024)(128)(4,1)S(1)} %broadcast_bitcast_fusion), kind=kLoop, calls=%fused_computation.3 | loop fusion | flops 20970496 | bytes 16789504 | tf_op jit(solution)/shard_map/reduce_sum | solution.py:56
  444.5 0.0 all-to-all-done
  444.5 10.5 %fusion.26 = bf16[128,8,128]{0,2,1:T(8,128)(2,1)S(1)} fusion(f32[8,128,4096]{2,1,0:T(8,128)} %get-tuple-element.10, f32[8,128]{1,0:T(8,128)S(1)} %get-tuple-element.8, pred[4096]{0:T(1024)(128)(4,1)S(1)} %broadcast_bitcast_fusion, f32[128,8]{0,1:T(8,128)S(1)} %bitcast.46, f32[128,8]{0,1:T(8,128)S(1)} %get-tuple-element.7, ...), kind=kOutput, calls=%fused_computation.15 | convolution fusion | flops 1095106560 | bytes 25444352 | tf_op jit(solution)/shard_map/hqk,khd->qhd/dot_general | solution.py:57
  455.0 0.9 copy.20
  (4 shorter events, 0.0 us)
Async XLA Ops:
  6.5 418.0 %copy-start = (bf16[128,1024]{1,0:T(8,128)(2,1)S(1)}, bf16[128,1024]{1,0:T(8,128)(2,1)}, u32[]{:S(2)}) copy-start(bf16[128,1024]{1,0:T(8,128)(2,1)} %param.6) | copy-start | bytes 786436
  6.5 37.2 %copy-start.2 = (s32[1,32]{1,0:T(1,128)S(1)}, s32[1,32]{1,0:T(1,128)}, u32[]{:S(2)}) copy-start(s32[1,32]{1,0:T(1,128)} %param.11) | copy-start | bytes 388
  6.5 418.0 %copy-start.1 = (f32[1024]{0:T(1024)S(1)}, f32[1024]{0:T(1024)}, u32[]{:S(2)}) copy-start(f32[1024]{0:T(1024)} %param.9) | copy-start | bytes 12292
  6.5 418.0 %all-gather.2.cloned.1.call-start = ((), (), s32[]{:S(2)}) async-start(), calls=%async_computation.1 | async-start | bytes 8650752 | tf_op jit(solution)/shard_map/all_gather | solution.py:40
  27.7 416.8 %all-to-all-start = ((bf16[32,128,8,128]{1,3,2,0:T(8,128)(2,1)}), bf16[32,128,8,128]{1,3,2,0:T(8,128)(2,1)}, u32[]{:S(2)}, u32[]{:S(2)}) async-start(bf16[32,128,8,128]{1,3,2,0:T(8,128)(2,1)} %stack.3), calls=%async_computation | async-start | bytes 16777216 | tf_op jit(solution)/shard_map/all_to_all | solution.py:43
Sparse Core Ops, SparseCore 0:
  21.4 403.1 all-gather.1
